TPU v7x, 256 devices: a whole 4x4x8 slice. The times are simulated.
256 devices in a mesh: src: 32 (over z, x), tgt: 8 (over y, core).
Axes of the slice: x: 4, y: 4, z: 8, core: 2. Of those that a mesh axis runs over, the one named last changes fastest.
Arguments:
- src_embed: float32 [65536, 256], P(('src', 'tgt')), may hold values from -7.5 to 7.5
- tgt_embed: float32 [32768, 256], P(('tgt', 'src')), may hold values from -7.5 to 7.5
- log_src: float32 [65536], P('src'), may hold values from -1.25 to 2.35
- log_tgt: float32 [32768], P('tgt'), may hold values from -1.25 to 2.35
- tgt_pot: float32 [32768], P('tgt'), may hold values from -1 to 6
Outputs:
- src_dual: float32 [65536], P('src')
- tgt_dual: float32 [32768], P('tgt')
All inputs are finite; a program needn't handle non-finite values.
Results may differ from a plain program's by a relative error of at most 0.0003.
Values sent between devices are 32-bit elements; how exact they have to be, the bound alone decides.
No kernel may reach another device: no remote copies, remote signals or barrier semaphores. Data moves between devices by JAX's collectives and lax.ppermute only.
A program may use at most 128 MiB of HBM per device.

v0:
```python
import jax
import jax.numpy as jnp
from jax import lax
from jax.sharding import PartitionSpec as P

EPSILON = 0.05


def cross_inner(left, right):
    return lax.dot_general(
        left,
        right,
        (((1,), (1,)), ((), ())),
        precision=lax.Precision.HIGHEST,
        preferred_element_type=jnp.float32,
    )


def row_lse(scores):
    highest = lax.pmax(jnp.max(scores, axis=1), "tgt")
    totals = lax.psum(jnp.sum(jnp.exp(scores - highest[:, None]), axis=1), "tgt")
    return highest + jnp.log(totals)


def column_lse(scores):
    highest = lax.pmax(jnp.max(scores, axis=0), "src")
    totals = lax.psum(jnp.sum(jnp.exp(scores - highest[None, :]), axis=0), "src")
    return highest + jnp.log(totals)


def shards(src_embed, tgt_embed, log_src, log_tgt, tgt_pot):
    width = src_embed.shape[1]
    targets = lax.all_gather(tgt_embed, "src", axis=0, tiled=True)
    tgt_norm = jnp.sum(targets * targets, axis=1)
    piece = lax.all_gather(src_embed, "tgt", axis=0, tiled=True)
    src_norm = jnp.sum(piece * piece, axis=1)
    cost = (src_norm[:, None] + tgt_norm[None, :] - 2.0 * cross_inner(piece, targets)) / width
    tgt_dual = tgt_pot
    src_dual = -EPSILON * row_lse(log_tgt[None, :] + (tgt_dual[None, :] - cost) / EPSILON)
    tgt_dual = -EPSILON * column_lse(log_src[:, None] + (src_dual[:, None] - cost) / EPSILON)
    return (src_dual, tgt_dual)


def solution(mesh):
    in_specs = (P(("src", "tgt"), None), P(("tgt", "src"), None), P("src"), P("tgt"), P("tgt"))
    out_specs = (P("src"), P("tgt"))
    return jax.shard_map(shards, mesh=mesh, in_specs=in_specs, out_specs=out_specs, check_vma=False)
```

profile of v0, /device:TPU:0, one launch (start us, length us, event | category | flops | bytes accessed | tf_op | source)
XLA Modules:
  0.0 522.3 jit_solution(12428725631582622613)
XLA Ops:
  7.2 0.0 all-gather.3.cloned.1.call-start
  7.2 0.7 all-gather.3.cloned.1.call-update
  7.9 0.0 all-gather.5.cloned.1.call-start
  7.9 0.7 all-gather.5.cloned.1.call-update
  8.6 30.4 %all-gather.3.cloned.1.call-done = f32[2048,256]{1,0:T(8,128)} async-done(((f32[256,256]{1,0:T(8,128)}), f32[2048,256]{1,0:T(8,128)}) %all-gather.3.cloned.1.call-update) | async-done | bytes 2097168 | tf_op jit(solution)/shard_map/all_gather | solution.py:35
  39.0 1.9 multiply_reduce_fusion.1
  40.9 82.8 %all-gather.5.cloned.1.call-done = f32[4096,256]{1,0:T(8,128)} async-done(((f32[128,256]{1,0:T(8,128)}), f32[4096,256]{1,0:T(8,128)}) %all-gather.5.cloned.1.call-update) | async-done | bytes 4194320 | tf_op jit(solution)/shard_map/all_gather | solution.py:33
  123.8 2.8 multiply_reduce_fusion
  126.6 0.0 copy-start.2
  126.6 0.0 copy-start.3
  126.6 41.2 %fusion = (f32[2048]{0:T(1024)S(1)}, f32[2048,4096]{1,0:T(8,128)}) fusion(f32[4096]{0:T(1024)} %param.9, f32[4096]{0:T(1024)} %param.8, f32[2048,256]{1,0:T(8,128)} %all-gather.3.cloned.1.call-done, f32[4096,256]{1,0:T(8,128)} %all-gather.5.cloned.1.call-done, f32[4096]{0:T(1024)S(1)} %multiply_reduce_fusion, f32[2048]{0:T(1024)S(1)} %multiply_reduce_fusion.1), kind=kOutput, calls=%fused_computation.5 | convolution fusion | flops 25836910592 | bytes 39911424 | tf_op jit(solution)/shard_map/dot_general | solution.py:10
  167.8 0.0 copy-start.1
  167.8 12.8 %pmax.14 = f32[2048]{0:T(1024)S(1)} all-reduce(f32[2048]{0:T(1024)S(1)} %get-tuple-element.2), channel_id=1, replica_groups=mesh['src'=32,'tgt'=8] {'tgt'}, use_global_device_ids=true, to_apply=%region_3.0 | all-reduce | flops 2048 | bytes 16384 | tf_op jit(solution)/shard_map/pmax | solution.py:20
  180.6 0.0 copy-done.2
  180.6 0.0 copy-done.3
  180.7 15.2 %exponential_reduce_fusion.1 = f32[2048]{0:T(1024)S(1)} fusion(f32[2048,4096]{1,0:T(8,128)} %get-tuple-element.3, f32[2048]{0:T(1024)S(1)} %pmax.14, f32[4096]{0:T(1024)S(1)} %copy-done.2, f32[4096]{0:T(1024)S(1)} %copy-done.3), kind=kLoop, calls=%fused_computation.2 | loop fusion | flops 41940992 | bytes 33603584 | tf_op jit(solution)/shard_map/reduce_sum | solution.py:21
  195.8 12.7 %psum.14 = f32[2048]{0:T(1024)S(1)} all-reduce(f32[2048]{0:T(1024)S(1)} %exponential_reduce_fusion.1), channel_id=1, replica_groups=mesh['src'=32,'tgt'=8] {'tgt'}, use_global_device_ids=true, to_apply=%region_5.0 | all-reduce | flops 2048 | bytes 16384 | tf_op jit(solution)/shard_map/psum | solution.py:21
  208.5 0.0 copy-done.1
  208.5 0.0 copy-start
  208.5 13.7 %fusion.1 = f32[4096]{0:T(1024)S(1)} fusion(f32[2048,4096]{1,0:T(8,128)} %get-tuple-element.3, f32[2048]{0:T(1024)S(1)} %add_multiply_fusion.1, f32[2048]{0:T(1024)S(1)} %copy-done.1), kind=kLoop, calls=%fused_computation.6 | loop fusion | flops 33550336 | bytes 33587200 | tf_op jit(solution)/shard_map/reduce_max | solution.py:26
  222.2 139.8 %pmax.15 = f32[4096]{0:T(1024)S(1)} all-reduce(f32[4096]{0:T(1024)S(1)} %fusion.1), channel_id=1, replica_groups=mesh['src'=32,'tgt'=8] {'src'}, use_global_device_ids=true, to_apply=%region_7.0 | all-reduce | flops 4096 | bytes 32768 | tf_op jit(solution)/shard_map/pmax | solution.py:26
  362.1 15.1 %exponential_reduce_fusion = f32[4096]{0:T(1024)S(1)} fusion(f32[2048,4096]{1,0:T(8,128)} %get-tuple-element.3, f32[4096]{0:T(1024)S(1)} %pmax.15, f32[2048]{0:T(1024)S(1)} %add_multiply_fusion.1, f32[2048]{0:T(1024)S(1)} %copy-done.1), kind=kLoop, calls=%fused_computation | loop fusion | flops 41938944 | bytes 33603584 | tf_op jit(solution)/shard_map/reduce_sum | solution.py:27
  377.2 0.0 copy-done
  377.2 137.7 %psum.15 = f32[4096]{0:T(1024)S(1)} all-reduce(f32[4096]{0:T(1024)S(1)} %exponential_reduce_fusion), channel_id=1, replica_groups=mesh['src'=32,'tgt'=8] {'src'}, use_global_device_ids=true, to_apply=%region_9.0 | all-reduce | flops 4096 | bytes 32768 | tf_op jit(solution)/shard_map/psum | solution.py:27
  514.9 0.6 add_multiply_fusion
  (1 shorter events, 0.0 us)
Async XLA Ops:
  7.2 31.8 %all-gather.3.cloned.1.call-start = ((), (), s32[]{:S(2)}) async-start(), calls=%async_computation | async-start | bytes 2359296 | tf_op jit(solution)/shard_map/all_gather | solution.py:35
  7.9 115.9 %all-gather.5.cloned.1.call-start = ((), (), s32[]{:S(2)}) async-start(), calls=%async_computation.1 | async-start | bytes 4325376 | tf_op jit(solution)/shard_map/all_gather | solution.py:33
  126.6 54.1 %copy-start.2 = (f32[4096]{0:T(1024)S(1)}, f32[4096]{0:T(1024)}, u32[]{:S(2)}) copy-start(f32[4096]{0:T(1024)} %param.9) | copy-start | bytes 49156
  126.6 54.1 %copy-start.3 = (f32[4096]{0:T(1024)S(1)}, f32[4096]{0:T(1024)}, u32[]{:S(2)}) copy-start(f32[4096]{0:T(1024)} %param.8) | copy-start | bytes 49156
  167.8 40.7 %copy-start.1 = (f32[2048]{0:T(1024)S(1)}, f32[2048]{0:T(1024)}, u32[]{:S(2)}) copy-start(f32[2048]{0:T(1024)} %param.7) | copy-start | bytes 24580
  208.5 168.7 %copy-start = (f32[2048]{0:T(1024)}, f32[2048]{0:T(1024)S(1)}, u32[]{:S(2)}) copy-start(f32[2048]{0:T(1024)S(1)} %add_multiply_fusion.1) | copy-start | bytes 24580
Sparse Core Ops, SparseCore 0:
  9.8 29.1 all-gather.2
  41.6 82.1 all-gather.4
where the time goes:
time: 523 us; the launch traced here: 522 us
  blocking collectives  303 us (58%)
  waiting for transfers between devices  115 us (22%)
  other arithmetic  49.3 us (9%)
  matrix products  41.2 us (8%)
  between operations  14.1 us (3%)
    pmax x1, blocking collectives, column_lse(): highest = lax.pmax(jnp.max(scores, axis=0), 'src')  140 us
    psum x1, blocking collectives, column_lse(): lax.psum(jnp.sum(jnp.exp(scores - highest[None, :]), axis=0), 'src')  138 us
    all_gather x1, waiting for transfers between devices, shards(): targets = lax.all_gather(tgt_embed, 'src', axis=0, tiled=True)  82.8 us
    dot_general x1, matrix products, cross_inner(): lax.dot_general(left, right, (((1,), (1,)), ((), ())), precision=lax.Prec...  41.2 us
    all_gather x1, waiting for transfers between devices, shards(): piece = lax.all_gather(src_embed, 'tgt', axis=0, tiled=True)  30.4 us
    reduce_sum x1, other arithmetic, row_lse(): jnp.sum(jnp.exp(scores - highest[:, None]), axis=1)  15.2 us
    reduce_sum x1, other arithmetic, column_lse(): jnp.sum(jnp.exp(scores - highest[None, :]), axis=0)  15.1 us
    reduce_max x1, other arithmetic, column_lse(): highest = lax.pmax(jnp.max(scores, axis=0), 'src')  13.7 us
  transfers between devices with their start and end apart: 2, of which 2 were waited for; matrix products, arithmetic and copies ran while one was open for 0% of the time, Pallas kernels for 0%

commit v1 on v0

--- a/solution.py
+++ b/solution.py
@@ -30,7 +30,9 @@
 
 def shards(src_embed, tgt_embed, log_src, log_tgt, tgt_pot):
     width = src_embed.shape[1]
-    targets = lax.all_gather(tgt_embed, "src", axis=0, tiled=True)
+    targets = jnp.concatenate(
+        lax.all_to_all(jnp.stack([tgt_embed] * lax.axis_size("src")), "src", 0, 0), axis=0
+    )
     tgt_norm = jnp.sum(targets * targets, axis=1)
     piece = lax.all_gather(src_embed, "tgt", axis=0, tiled=True)
     src_norm = jnp.sum(piece * piece, axis=1)

time: 523 us -> 516 us (0.987)
  waiting for transfers between devices: 115 us -> 92.3 us
  starting transfers between devices: 0.08 us -> 9.78 us
    all_gather x1 -> x0, waiting for transfers between devices: 82.8 us -> none  [shards(): targets = lax.all_gather(tgt_embed, 'src', axis=0, tiled=True)]
    all_to_all x0 -> x1, waiting for transfers between devices: none -> 60.4 us  [shards(): lax.all_to_all(jnp.stack([tgt_embed] * lax.axis_size('src')), 'src', 0, 0)]
    all_to_all x0 -> x1, starting transfers between devices: none -> 9.74 us  [shards(): lax.all_to_all(jnp.stack([tgt_embed] * lax.axis_size('src')), 'src', 0, 0)]
where the time goes in v1:
time: 516 us; the launch traced here: 515 us
  blocking collectives  305 us (59%)
  waiting for transfers between devices  92.3 us (18%)
  other arithmetic  49.3 us (10%)
  matrix products  41.2 us (8%)
  between operations  14.1 us (3%)
  starting transfers between devices  9.78 us (2%)
    pmax x1, blocking collectives, column_lse(): highest = lax.pmax(jnp.max(scores, axis=0), 'src')  141 us
    psum x1, blocking collectives, column_lse(): lax.psum(jnp.sum(jnp.exp(scores - highest[None, :]), axis=0), 'src')  138 us
    all_to_all x1, waiting for transfers between devices, shards(): lax.all_to_all(jnp.stack([tgt_embed] * lax.axis_size('src')), 'src', 0, 0)  60.4 us
    dot_general x1, matrix products, cross_inner(): lax.dot_general(left, right, (((1,), (1,)), ((), ())), precision=lax.Prec...  41.2 us
    all_gather x1, waiting for transfers between devices, shards(): piece = lax.all_gather(src_embed, 'tgt', axis=0, tiled=True)  31.2 us
    reduce_sum x1, other arithmetic, row_lse(): jnp.sum(jnp.exp(scores - highest[:, None]), axis=1)  15.2 us
    reduce_sum x1, other arithmetic, column_lse(): jnp.sum(jnp.exp(scores - highest[None, :]), axis=0)  15.1 us
    pmax x1, blocking collectives, row_lse(): highest = lax.pmax(jnp.max(scores, axis=1), 'tgt')  13.8 us
  transfers between devices with their start and end apart: 2, of which 2 were waited for; matrix products, arithmetic and copies ran while one was open for 0% of the time, Pallas kernels for 0%

profile of v1, /device:TPU:0, one launch (start us, length us, event | category | flops | bytes accessed | tf_op | source)
XLA Modules:
  0.0 514.9 jit_solution(18314471034097444825)
XLA Ops:
  7.2 3.3 stack.2
  10.5 9.7 %all-to-all-start = ((f32[32,128,256]{2,1,0:T(8,128)}), f32[32,128,256]{2,1,0:T(8,128)}, u32[]{:S(2)}, u32[]{:S(2)}) async-start(f32[32,128,256]{2,1,0:T(8,128)} %stack.2), calls=%async_computation | async-start | bytes 8388608 | tf_op jit(solution)/shard_map/all_to_all | solution.py:34
  20.2 0.0 all-gather.2.cloned.1.call-start
  20.3 0.7 all-gather.2.cloned.1.call-update
  20.9 31.2 %all-gather.2.cloned.1.call-done = f32[2048,256]{1,0:T(8,128)} async-done(((f32[256,256]{1,0:T(8,128)}), f32[2048,256]{1,0:T(8,128)}) %all-gather.2.cloned.1.call-update) | async-done | bytes 2097168 | tf_op jit(solution)/shard_map/all_gather | solution.py:37
  52.1 1.9 multiply_reduce_fusion.1
  54.1 60.4 %all-to-all-done = f32[32,128,256]{2,1,0:T(8,128)} async-done(((f32[32,128,256]{2,1,0:T(8,128)}), f32[32,128,256]{2,1,0:T(8,128)}, u32[]{:S(2)}, u32[]{:S(2)}) %all-to-all-start) | async-done | bytes 4194336 | tf_op jit(solution)/shard_map/all_to_all | solution.py:34
  114.5 2.8 multiply_reduce_fusion
  117.3 0.0 copy-start.2
  117.3 0.0 copy-start.3
  117.3 41.2 %fusion = (f32[2048]{0:T(1024)S(1)}, f32[2048,4096]{1,0:T(8,128)}) fusion(f32[4096]{0:T(1024)} %param.9, f32[4096]{0:T(1024)} %param.8, f32[2048,256]{1,0:T(8,128)} %all-gather.2.cloned.1.call-done, f32[4096,256]{1,0:T(8,128)} %bitcast.1, f32[4096]{0:T(1024)S(1)} %bitcast.4, f32[2048]{0:T(1024)S(1)} %multiply_reduce_fusion.1), kind=kOutput, calls=%fused_computation.5 | convolution fusion | flops 25836910592 | bytes 39911424 | tf_op jit(solution)/shard_map/dot_general | solution.py:10
  158.5 0.0 copy-start.1
  158.5 13.8 %pmax.14 = f32[2048]{0:T(1024)S(1)} all-reduce(f32[2048]{0:T(1024)S(1)} %get-tuple-element.2), channel_id=1, replica_groups=mesh['src'=32,'tgt'=8] {'tgt'}, use_global_device_ids=true, to_apply=%region_3.0 | all-reduce | flops 2048 | bytes 16384 | tf_op jit(solution)/shard_map/pmax | solution.py:20
  172.3 0.0 copy-done.2
  172.3 0.0 copy-done.3
  172.3 15.2 %exponential_reduce_fusion.1 = f32[2048]{0:T(1024)S(1)} fusion(f32[2048,4096]{1,0:T(8,128)} %get-tuple-element.3, f32[2048]{0:T(1024)S(1)} %pmax.14, f32[4096]{0:T(1024)S(1)} %copy-done.2, f32[4096]{0:T(1024)S(1)} %copy-done.3), kind=kLoop, calls=%fused_computation.2 | loop fusion | flops 41940992 | bytes 33603584 | tf_op jit(solution)/shard_map/reduce_sum | solution.py:21
  187.5 12.7 %psum.14 = f32[2048]{0:T(1024)S(1)} all-reduce(f32[2048]{0:T(1024)S(1)} %exponential_reduce_fusion.1), channel_id=1, replica_groups=mesh['src'=32,'tgt'=8] {'tgt'}, use_global_device_ids=true, to_apply=%region_5.0 | all-reduce | flops 2048 | bytes 16384 | tf_op jit(solution)/shard_map/psum | solution.py:21
  200.2 0.0 copy-done.1
  200.2 0.0 copy-start
  200.2 13.7 %fusion.1 = f32[4096]{0:T(1024)S(1)} fusion(f32[2048,4096]{1,0:T(8,128)} %get-tuple-element.3, f32[2048]{0:T(1024)S(1)} %add_multiply_fusion.1, f32[2048]{0:T(1024)S(1)} %copy-done.1), kind=kLoop, calls=%fused_computation.6 | loop fusion | flops 33550336 | bytes 33587200 | tf_op jit(solution)/shard_map/reduce_max | solution.py:26
  213.9 140.7 %pmax.15 = f32[4096]{0:T(1024)S(1)} all-reduce(f32[4096]{0:T(1024)S(1)} %fusion.1), channel_id=1, replica_groups=mesh['src'=32,'tgt'=8] {'src'}, use_global_device_ids=true, to_apply=%region_7.0 | all-reduce | flops 4096 | bytes 32768 | tf_op jit(solution)/shard_map/pmax | solution.py:26
  354.7 15.1 %exponential_reduce_fusion = f32[4096]{0:T(1024)S(1)} fusion(f32[2048,4096]{1,0:T(8,128)} %get-tuple-element.3, f32[4096]{0:T(1024)S(1)} %pmax.15, f32[2048]{0:T(1024)S(1)} %add_multiply_fusion.1, f32[2048]{0:T(1024)S(1)} %copy-done.1), kind=kLoop, calls=%fused_computation | loop fusion | flops 41938944 | bytes 33603584 | tf_op jit(solution)/shard_map/reduce_sum | solution.py:27
  369.8 0.0 copy-done
  369.8 137.7 %psum.15 = f32[4096]{0:T(1024)S(1)} all-reduce(f32[4096]{0:T(1024)S(1)} %exponential_reduce_fusion), channel_id=1, replica_groups=mesh['src'=32,'tgt'=8] {'src'}, use_global_device_ids=true, to_apply=%region_9.0 | all-reduce | flops 4096 | bytes 32768 | tf_op jit(solution)/shard_map/psum | solution.py:27
  507.4 0.6 add_multiply_fusion
  (1 shorter events, 0.0 us)
Async XLA Ops:
  10.5 104.0 %all-to-all-start = ((f32[32,128,256]{2,1,0:T(8,128)}), f32[32,128,256]{2,1,0:T(8,128)}, u32[]{:S(2)}, u32[]{:S(2)}) async-start(f32[32,128,256]{2,1,0:T(8,128)} %stack.2), calls=%async_computation | async-start | bytes 8388608 | tf_op jit(solution)/shard_map/all_to_all | solution.py:34
  20.2 31.9 %all-gather.2.cloned.1.call-start = ((), (), s32[]{:S(2)}) async-start(), calls=%async_computation.1 | async-start | bytes 2359296 | tf_op jit(solution)/shard_map/all_gather | solution.py:37
  117.3 55.0 %copy-start.2 = (f32[4096]{0:T(1024)S(1)}, f32[4096]{0:T(1024)}, u32[]{:S(2)}) copy-start(f32[4096]{0:T(1024)} %param.9) | copy-start | bytes 49156
  117.3 55.0 %copy-start.3 = (f32[4096]{0:T(1024)S(1)}, f32[4096]{0:T(1024)}, u32[]{:S(2)}) copy-start(f32[4096]{0:T(1024)} %param.8) | copy-start | bytes 49156
  158.5 41.7 %copy-start.1 = (f32[2048]{0:T(1024)S(1)}, f32[2048]{0:T(1024)}, u32[]{:S(2)}) copy-start(f32[2048]{0:T(1024)} %param.7) | copy-start | bytes 24580
  200.2 169.6 %copy-start = (f32[2048]{0:T(1024)}, f32[2048]{0:T(1024)S(1)}, u32[]{:S(2)}) copy-start(f32[2048]{0:T(1024)S(1)} %add_multiply_fusion.1) | copy-start | bytes 24580
Sparse Core Ops, SparseCore 0:
  22.9 29.2 all-gather.1
